TPU v7x, 512 devices: a whole 4x4x16 slice. The times are simulated.
512 devices in a mesh: dp: 64 (over z, x_lo, core), head: 8 (over x_hi, y).
Axes of the slice: x: 4 (x_hi: 2, x_lo: 2; x = x_hi * 2 + x_lo), y: 4, z: 16, core: 2. Of those that a mesh axis runs over, the one named last changes fastest.
Arguments:
- layer_input: bfloat16 [65536, 8192], P('dp', 'head'), may hold values from -0.09375 to 0.09375
- query_states: bfloat16 [65536, 4096], P(('dp', 'head')), may hold values from -7.5 to 7.5
- key_states: bfloat16 [65536, 1024], P(('dp', 'head')), may hold values from -6 to 6
- value_states: bfloat16 [65536, 1024], P(('dp', 'head')), may hold values from -6 to 6
- out_grad: bfloat16 [65536, 4096], P(('dp', 'head')), may hold values from -6 to 6
- parents: int32 [65536], P('dp'), may hold values from 0 to 510, as said below
- lengths: int32 [128], P('dp'), may hold values from 1 to 512, 40960 in all
Outputs:
- weight_gradient: float32 [1024, 8192], P('dp', 'head')
- value_gradient: bfloat16 [65536, 1024], P(('dp', 'head'))
Inputs may be any that keep to these rules, and one draw needn't show every extreme that they name: `parents`: within each tree a token's parent is an earlier token of the same tree; the first token of a tree is its own parent. The lengths of all trees sum to 40960.
All inputs are finite; a program needn't handle non-finite values. No bound on the sum of `lengths` on one device may be relied on, other than what follows from the above.
Results may differ from a plain program's by a relative error of at most 0.0049.
Values may be sent and summed in bfloat16 or wider, within the bound.
No kernel may reach another device: no remote copies, remote signals or barrier semaphores. Data moves between devices by JAX's collectives and lax.ppermute only.
A program may use at most 64 MiB of HBM per device.

v0:
```python
import jax
import jax.numpy as jnp
from jax import lax
from jax.sharding import PartitionSpec as P

HEAD_DIM = 128
TREE_LEN = 512


def ancestry_of(parent_tree):
    slots = parent_tree.shape[0]
    positions = jnp.arange(slots, dtype=jnp.int32)
    reached = positions[:, None] == positions[None, :]
    jumps = parent_tree
    for number in range(max(1, (slots - 1).bit_length())):
        reached = reached | reached[jumps]
        jumps = jumps[jumps]
    return reached


def block_grads(query_part, grad_part, key_heads, value_heads, live_pairs):
    scaling = HEAD_DIM ** (-0.5)
    scores = (
        jnp.einsum("ikgd,jkd->kgij", query_part, key_heads, preferred_element_type=jnp.float32)
        * scaling
    )
    masked = jnp.where(live_pairs, scores, jnp.float32(-1e30))
    maxima = jnp.max(masked, axis=-1, keepdims=True)
    exponent = jnp.where(live_pairs, jnp.exp(masked - maxima), jnp.float32(0.0))
    row_sums = jnp.sum(exponent, axis=-1, keepdims=True)
    softmax_weights = exponent / jnp.maximum(row_sums, 1.0)
    value_scores = jnp.einsum(
        "ikgd,jkd->kgij", grad_part, value_heads, preferred_element_type=jnp.float32
    )
    row_dots = jnp.sum(softmax_weights * value_scores, axis=-1, keepdims=True)
    score_grads = (softmax_weights * (value_scores - row_dots) * scaling).astype(jnp.bfloat16)
    key_part = jnp.einsum(
        "kgij,ikgd->jkd", score_grads, query_part, preferred_element_type=jnp.float32
    )
    value_part = jnp.einsum(
        "kgij,ikgd->jkd",
        softmax_weights.astype(jnp.bfloat16),
        grad_part,
        preferred_element_type=jnp.float32,
    )
    return (key_part, value_part)


def tree_grads(query_tree, grad_tree, key_tree, value_tree, parent_tree, tree_length):
    kv_local = key_tree.shape[1] // HEAD_DIM
    groups = query_tree.shape[1] // key_tree.shape[1]
    query_heads = query_tree.reshape(TREE_LEN, kv_local, groups, HEAD_DIM)
    grad_heads = grad_tree.reshape(TREE_LEN, kv_local, groups, HEAD_DIM)
    key_heads = key_tree.reshape(TREE_LEN, kv_local, HEAD_DIM)
    value_heads = value_tree.reshape(TREE_LEN, kv_local, HEAD_DIM)
    ancestry = ancestry_of(parent_tree)
    positions = jnp.arange(TREE_LEN, dtype=jnp.int32)
    live_pairs = ancestry & (positions < tree_length)[:, None]
    key_sum, value_sum = block_grads(query_heads, grad_heads, key_heads, value_heads, live_pairs)
    return (
        key_sum.astype(jnp.bfloat16).reshape(TREE_LEN, kv_local * HEAD_DIM),
        value_sum.astype(jnp.bfloat16).reshape(TREE_LEN, kv_local * HEAD_DIM),
    )


def local(layer_input, query_states, key_states, value_states, out_grad, parents, lengths):
    queries, grads_out, keys_here, values_here = (
        lax.all_to_all(query_states, "head", split_axis=1, concat_axis=0, tiled=True),
        lax.all_to_all(out_grad, "head", split_axis=1, concat_axis=0, tiled=True),
        lax.all_to_all(key_states, "head", split_axis=1, concat_axis=0, tiled=True),
        lax.all_to_all(value_states, "head", split_axis=1, concat_axis=0, tiled=True),
    )
    trees = lengths.shape[0]
    stacked = (
        queries.reshape(trees, TREE_LEN, -1),
        grads_out.reshape(trees, TREE_LEN, -1),
        keys_here.reshape(trees, TREE_LEN, -1),
        values_here.reshape(trees, TREE_LEN, -1),
        parents.reshape(trees, TREE_LEN),
        lengths,
    )
    key_grads, value_grads = lax.map(lambda items: tree_grads(*items), stacked)
    key_grads = key_grads.reshape(trees * TREE_LEN, -1)
    value_grads = value_grads.reshape(trees * TREE_LEN, -1)
    key_all = lax.all_gather(key_grads, "head", axis=1, tiled=True)
    weight_gradient = lax.psum_scatter(
        lax.dot_general(
            key_all, layer_input, (((0,), (0,)), ((), ())), preferred_element_type=jnp.float32
        ),
        "dp",
        scatter_dimension=0,
        tiled=True,
    )
    value_gradient = lax.all_to_all(value_grads, "head", split_axis=0, concat_axis=1, tiled=True)
    return (weight_gradient, value_gradient)


def solution(mesh):
    placed = (
        P("dp", "head"),
        P(("dp", "head"), None),
        P(("dp", "head"), None),
        P(("dp", "head"), None),
        P(("dp", "head"), None),
        P("dp"),
        P("dp"),
    )
    return jax.shard_map(
        local,
        mesh=mesh,
        in_specs=placed,
        out_specs=(P("dp", "head"), P(("dp", "head"), None)),
        check_vma=False,
    )
```

profile of v0, /device:TPU:8, one launch (start us, length us, event | category | flops | bytes accessed | tf_op | source)
XLA Modules:
  0.0 527.1 jit_solution(8759982383548423130)
XLA Ops:
  7.2 1.8 copy_bitcast_fusion.1
  9.0 9.7 %all-to-all-start.1 = ((bf16[128,8,128]{2,0,1:T(8,128)(2,1)}), bf16[128,8,128]{2,0,1:T(8,128)(2,1)}, u32[]{:S(2)}, u32[]{:S(2)}) async-start(bf16[128,8,128]{2,0,1:T(8,128)(2,1)} %copy_bitcast_fusion.1), calls=%async_computation.1 | async-start | bytes 524288 | tf_op jit(solution)/shard_map/all_to_all | solution.py:70
  18.7 2.3 copy.45
  21.0 4.8 all-to-all-done.1
  25.8 5.3 all-to-all-start
  31.1 2.3 copy.49
  33.4 8.8 %all-to-all-done = bf16[128,8,512]{0,2,1:T(8,128)(2,1)S(1)} async-done(((bf16[128,8,512]{0,2,1:T(8,128)(2,1)}), bf16[128,8,512]{0,2,1:T(8,128)(2,1)S(1)}, u32[]{:S(2)}, u32[]{:S(2)}) %all-to-all-start) | async-done | bytes 1048608 | tf_op jit(solution)/shard_map/all_to_all | solution.py:68
  42.2 5.7 %all-to-all-start.3 = ((bf16[128,8,512]{0,2,1:T(8,128)(2,1)}), bf16[128,8,512]{0,2,1:T(8,128)(2,1)}, u32[]{:S(2)}, u32[]{:S(2)}) async-start(bf16[128,8,512]{0,2,1:T(8,128)(2,1)} %bitcast.261), calls=%async_computation.3 | async-start | bytes 2097152 | tf_op jit(solution)/shard_map/all_to_all | solution.py:69
  48.6 12.5 %all-to-all-done.3 = bf16[128,8,512]{0,2,1:T(8,128)(2,1)} async-done(((bf16[128,8,512]{0,2,1:T(8,128)(2,1)}), bf16[128,8,512]{0,2,1:T(8,128)(2,1)}, u32[]{:S(2)}, u32[]{:S(2)}) %all-to-all-start.3) | async-done | bytes 1048608 | tf_op jit(solution)/shard_map/all_to_all | solution.py:69
  61.1 5.4 %all-to-all-start.2 = ((bf16[128,8,128]{2,0,1:T(8,128)(2,1)}), bf16[128,8,128]{2,0,1:T(8,128)(2,1)}, u32[]{:S(2)}, u32[]{:S(2)}) async-start(bf16[128,8,128]{2,0,1:T(8,128)(2,1)} %copy_bitcast_fusion), calls=%async_computation.2 | async-start | bytes 524288 | tf_op jit(solution)/shard_map/all_to_all | solution.py:71
  67.1 1.3 copy.46
  68.4 2.3 copy.50
  70.7 2.9 all-to-all-done.2
  73.6 134.2 %while.12 = (s32[]{:T(128)}, bf16[2,512,128]{2,1,0:T(8,128)(2,1)}, bf16[2,512,128]{2,1,0:T(8,128)(2,1)}, bf16[2,512,512]{2,1,0:T(8,128)(2,1)}, s32[2,512]{1,0:T(...) while((s32[]{:T(128)}, bf16[2,512,128]{2,1,0:T(8,128)(2,1)}, ...), condition=%wide.region_4.5_spmd, body=%wide.region_0.4_spmd.sunk | while | flops 1109019648 | bytes 93070192 | solution.py:82
  74.3 3.5 gather_fusion.1
  77.9 1.8 gather_fusion
  79.8 1.8 gather_fusion.2
  81.7 3.5 gather_fusion.3
  85.3 1.8 gather_fusion.4
  87.2 3.5 gather_fusion.5
  90.8 1.8 gather_fusion.6
  92.7 3.5 gather_fusion.7
  96.2 1.8 gather_fusion.8
  98.2 3.5 gather_fusion.9
  101.7 1.8 gather_fusion.10
  103.7 3.5 gather_fusion.11
  107.2 1.8 gather_fusion.12
  109.2 3.5 gather_fusion.13
  112.7 1.8 gather_fusion.14
  114.7 3.5 gather_fusion.15
  118.2 1.8 gather_fusion.16
  121.8 1.1 constant_dynamic-slice_fusion.7
  123.2 1.9 fusion.81
  125.0 1.9 copy-done.1
  129.1 4.2 fusion.84
  133.4 1.9 fusion.85
  135.5 3.7 fusion.83
  141.4 3.5 gather_fusion.1
  145.0 1.8 gather_fusion
  146.9 1.8 gather_fusion.2
  148.9 3.5 gather_fusion.3
  152.4 1.8 gather_fusion.4
  154.3 3.5 gather_fusion.5
  157.9 1.8 gather_fusion.6
  159.8 3.5 gather_fusion.7
  163.3 1.8 gather_fusion.8
  165.3 3.5 gather_fusion.9
  168.8 1.8 gather_fusion.10
  170.8 3.5 gather_fusion.11
  174.3 1.8 gather_fusion.12
  176.3 3.5 gather_fusion.13
  179.8 1.8 gather_fusion.14
  181.8 3.5 gather_fusion.15
  185.3 1.8 gather_fusion.16
  189.0 1.1 constant_dynamic-slice_fusion.7
  190.3 1.9 fusion.81
  192.1 1.9 copy-done.1
  196.2 4.2 fusion.84
  200.5 1.9 fusion.85
  202.6 3.7 fusion.83
  207.9 71.3 %all-gather.2.cloned.1.call-done = bf16[1024,1024]{1,0:T(8,128)(2,1)} async-done(((bf16[1024,128]{1,0:T(8,128)(2,1)}), bf16[1024,1024]{1,0:T(8,128)(2,1)}) %all-gather.2.cloned.1.call-update) | async-done | bytes 2097168 | tf_op jit(solution)/shard_map/all_gather | solution.py:85
  279.1 5.9 %fusion.51 = f32[1024,1024]{1,0:T(8,128)} fusion(bf16[1024,1024]{1,0:T(8,128)(2,1)} %all-gather.2.cloned.1.call-done, bf16[1024,1024]{1,0:T(8,128)(2,1)S(1)} %copy-done), kind=kOutput, calls=%fused_computation.86 | convolution fusion | flops 2147483648 | bytes 8388608 | tf_op jit(solution)/shard_map/dot_general | solution.py:87
  286.0 11.2 %all_to_all.83 = bf16[8,128,128]{2,1,0:T(8,128)(2,1)S(1)} all-to-all(bf16[8,128,128]{2,1,0:T(8,128)(2,1)S(1)} %bitcast.265), channel_id=1, replica_groups=mesh['dp'=64,'head'=8] {'head'}, dimensions={0} | all-to-all | bytes 524288 | tf_op jit(solution)/shard_map/all_to_all | solution.py:94
  298.3 222.0 %reduce-scatter.2.cloned.1.call-done = f32[16,1024]{1,0:T(8,128)} async-done(((f32[1024,1024]{1,0:T(8,128)}), f32[16,1024]{1,0:T(8,128)}) %reduce-scatter.2.cloned.1.call-update) | async-done | bytes 65552 | tf_op jit(solution)/shard_map/reduce_scatter | solution.py:86
  (124 shorter events, 19.6 us)
Async XLA Ops:
  7.2 271.9 %copy-start = (bf16[1024,1024]{1,0:T(8,128)(2,1)S(1)}, bf16[1024,1024]{1,0:T(8,128)(2,1)}, u32[]{:S(2)}) copy-start(bf16[1024,1024]{1,0:T(8,128)(2,1)} %param.9) | copy-start | bytes 6291460
  9.0 16.8 %all-to-all-start.1 = ((bf16[128,8,128]{2,0,1:T(8,128)(2,1)}), bf16[128,8,128]{2,0,1:T(8,128)(2,1)}, u32[]{:S(2)}, u32[]{:S(2)}) async-start(bf16[128,8,128]{2,0,1:T(8,128)(2,1)} %copy_bitcast_fusion.1), calls=%async_computation.1 | async-start | bytes 524288 | tf_op jit(solution)/shard_map/all_to_all | solution.py:70
  18.7 29.1 %copy-start.5 = (bf16[128,1024]{1,0:T(8,128)(2,1)S(1)}, bf16[128,1024]{1,0:T(8,128)(2,1)}, u32[]{:S(2)}) copy-start(bf16[128,1024]{1,0:T(8,128)(2,1)} %param.12) | copy-start | bytes 786436
  21.0 45.5 %copy-start.9 = (s32[1024]{0:T(1024)S(1)}, s32[1024]{0:T(1024)}, u32[]{:S(2)}) copy-start(s32[1024]{0:T(1024)} %param.14) | copy-start | bytes 12292
  25.8 16.4 %all-to-all-start = ((bf16[128,8,512]{0,2,1:T(8,128)(2,1)}), bf16[128,8,512]{0,2,1:T(8,128)(2,1)S(1)}, u32[]{:S(2)}, u32[]{:S(2)}) async-start(bf16[128,8,512]{0,2,1:T(8,128)(2,1)} %bitcast.260), calls=%async_computation | async-start | bytes 2097152 | tf_op jit(solution)/shard_map/all_to_all | solution.py:68
  33.4 40.2 %copy-start.10 = (s32[2]{0:T(128)S(1)}, s32[2]{0:T(128)}, u32[]{:S(2)}) copy-start(s32[2]{0:T(128)} %param.15) | copy-start | bytes 28
  42.2 19.0 %all-to-all-start.3 = ((bf16[128,8,512]{0,2,1:T(8,128)(2,1)}), bf16[128,8,512]{0,2,1:T(8,128)(2,1)}, u32[]{:S(2)}, u32[]{:S(2)}) async-start(bf16[128,8,512]{0,2,1:T(8,128)(2,1)} %bitcast.261), calls=%async_computation.3 | async-start | bytes 2097152 | tf_op jit(solution)/shard_map/all_to_all | solution.py:69
  61.1 12.4 %all-to-all-start.2 = ((bf16[128,8,128]{2,0,1:T(8,128)(2,1)}), bf16[128,8,128]{2,0,1:T(8,128)(2,1)}, u32[]{:S(2)}, u32[]{:S(2)}) async-start(bf16[128,8,128]{2,0,1:T(8,128)(2,1)} %copy_bitcast_fusion), calls=%async_computation.2 | async-start | bytes 524288 | tf_op jit(solution)/shard_map/all_to_all | solution.py:71
  66.5 212.6 %all-gather.2.cloned.1.call-start = ((), (), s32[]{:S(2)}) async-start(), calls=%async_computation.6 | async-start | bytes 2359296 | tf_op jit(solution)/shard_map/all_gather | solution.py:85
  123.1 4.9 copy-start.4
  125.0 2.0 copy-start.1
  129.1 4.3 copy-start.2
  133.4 2.1 copy-start.3
  135.4 3.8 copy-start.6
  135.4 5.2 copy-start.11
  140.0 0.7 copy-start.7
  190.3 4.9 copy-start.4
  192.1 2.0 copy-start.1
  196.2 4.3 copy-start.2
  200.5 2.1 copy-start.3
  202.5 3.8 copy-start.6
  202.6 5.2 copy-start.11
  207.1 0.7 copy-start.7
  207.8 312.5 %reduce-scatter.2.cloned.1.call-start = ((), (), s32[]{:S(2)}) async-start(), calls=%async_computation.7 | async-start | bytes 4259840 | tf_op jit(solution)/shard_map/reduce_scatter | solution.py:86
  285.0 0.9 copy-start.8
Sparse Core Ops, SparseCore 0:
  207.9 71.1 all-gather.1
  285.2 235.0 reduce-scatter.1
where the time goes:
time: 528 us; the launch traced here: 527 us
  waiting for transfers between devices  322 us (61%)
  local copies, waits for them, and re-layouts  115 us (22%)
  matrix products  29.4 us (6%)
  starting transfers between devices  26.1 us (5%)
  between operations  14.1 us (3%)
  blocking collectives  11.2 us (2%)
  other arithmetic  8.39 us (2%)
    reduce_scatter x1, waiting for transfers between devices, local(): lax.psum_scatter(lax.dot_general(key_all, layer_input, (((0,), (0,)), (()...  222 us
    all_gather x1, waiting for transfers between devices, local(): key_all = lax.all_gather(key_grads, 'head', axis=1, tiled=True)  71.3 us
    gather x16, local copies, waits for them, and re-layouts, ancestry_of(): jumps = jumps[jumps]  55.9 us
    gather x18, local copies, waits for them, and re-layouts, ancestry_of(): reached = reached | reached[jumps]  31.8 us
    all_to_all x1, waiting for transfers between devices, local(): lax.all_to_all(out_grad, 'head', split_axis=1, concat_axis=0, tiled=True)  12.5 us
    all_to_all x1, blocking collectives, local(): lax.all_to_all(value_grads, 'head', split_axis=0, concat_axis=1, tiled=True)  11.2 us
  transfers between devices with their start and end apart: 6, of which 6 were waited for; matrix products, arithmetic and copies ran while one was open for 2% of the time, Pallas kernels for 0%

commit v1 on v0

--- a/solution.py
+++ b/solution.py
@@ -82,7 +82,9 @@
     key_grads, value_grads = lax.map(lambda items: tree_grads(*items), stacked)
     key_grads = key_grads.reshape(trees * TREE_LEN, -1)
     value_grads = value_grads.reshape(trees * TREE_LEN, -1)
-    key_all = lax.all_gather(key_grads, "head", axis=1, tiled=True)
+    key_all = jnp.concatenate(
+        lax.all_to_all(jnp.stack([key_grads] * lax.axis_size("head")), "head", 0, 0), axis=1
+    )
     weight_gradient = lax.psum_scatter(
         lax.dot_general(
             key_all, layer_input, (((0,), (0,)), ((), ())), preferred_element_type=jnp.float32

time: 528 us -> 491 us (0.930)
  waiting for transfers between devices: 322 us -> 255 us
  blocking collectives: 11.2 us -> 41.5 us
    all_gather x1 -> x0, waiting for transfers between devices: 71.3 us -> none  [local(): key_all = lax.all_gather(key_grads, 'head', axis=1, tiled=True)]
    all_to_all x0 -> x1, blocking collectives: none -> 30.2 us  [local(): lax.all_to_all(jnp.stack([key_grads] * lax.axis_size('head')), 'head', 0, 0)]
  transfers between devices with their start and end apart: 6 -> 5, of which waited for: 6 -> 5; matrix products, arithmetic and copies ran while one was open for 2% -> 2% of each run, Pallas kernels for 0% -> 0%
where the time goes in v1:
time: 491 us; the launch traced here: 490 us
  waiting for transfers between devices  255 us (52%)
  local copies, waits for them, and re-layouts  116 us (24%)
  blocking collectives  41.5 us (8%)
  matrix products  27.8 us (6%)
  starting transfers between devices  26 us (5%)
  between operations  14.1 us (3%)
  other arithmetic  8.38 us (2%)
    reduce_scatter x1, waiting for transfers between devices, local(): lax.psum_scatter(lax.dot_general(key_all, layer_input, (((0,), (0,)), (()...  226 us
    gather x16, local copies, waits for them, and re-layouts, ancestry_of(): jumps = jumps[jumps]  55.9 us
    gather x18, local copies, waits for them, and re-layouts, ancestry_of(): reached = reached | reached[jumps]  31.8 us
    all_to_all x1, blocking collectives, local(): lax.all_to_all(jnp.stack([key_grads] * lax.axis_size('head')), 'head', 0, 0)  30.2 us
    all_to_all x1, waiting for transfers between devices, local(): lax.all_to_all(out_grad, 'head', split_axis=1, concat_axis=0, tiled=True)  12.5 us
    all_to_all x1, blocking collectives, local(): lax.all_to_all(value_grads, 'head', split_axis=0, concat_axis=1, tiled=True)  11.3 us
  transfers between devices with their start and end apart: 5, of which 5 were waited for; matrix products, arithmetic and copies ran while one was open for 2% of the time, Pallas kernels for 0%

profile of v1, /device:TPU:8, one launch (start us, length us, event | category | flops | bytes accessed | tf_op | source)
XLA Modules:
  0.0 489.9 jit_solution(13390739025187895570)
XLA Ops:
  7.2 1.8 copy_bitcast_fusion.1
  9.0 9.7 %all-to-all-start.1 = ((bf16[128,8,128]{2,0,1:T(8,128)(2,1)}), bf16[128,8,128]{2,0,1:T(8,128)(2,1)}, u32[]{:S(2)}, u32[]{:S(2)}) async-start(bf16[128,8,128]{2,0,1:T(8,128)(2,1)} %copy_bitcast_fusion.1), calls=%async_computation.1 | async-start | bytes 524288 | tf_op jit(solution)/shard_map/all_to_all | solution.py:70
  18.7 2.3 copy.47
  21.1 4.8 all-to-all-done.1
  25.8 5.3 %all-to-all-start = ((bf16[128,8,512]{0,2,1:T(8,128)(2,1)}), bf16[128,8,512]{0,2,1:T(8,128)(2,1)S(1)}, u32[]{:S(2)}, u32[]{:S(2)}) async-start(bf16[128,8,512]{0,2,1:T(8,128)(2,1)} %bitcast.263), calls=%async_computation | async-start | bytes 2097152 | tf_op jit(solution)/shard_map/all_to_all | solution.py:68
  31.1 2.3 copy.51
  33.4 8.8 %all-to-all-done = bf16[128,8,512]{0,2,1:T(8,128)(2,1)S(1)} async-done(((bf16[128,8,512]{0,2,1:T(8,128)(2,1)}), bf16[128,8,512]{0,2,1:T(8,128)(2,1)S(1)}, u32[]{:S(2)}, u32[]{:S(2)}) %all-to-all-start) | async-done | bytes 1048608 | tf_op jit(solution)/shard_map/all_to_all | solution.py:68
  42.2 5.7 %all-to-all-start.3 = ((bf16[128,8,512]{0,2,1:T(8,128)(2,1)}), bf16[128,8,512]{0,2,1:T(8,128)(2,1)}, u32[]{:S(2)}, u32[]{:S(2)}) async-start(bf16[128,8,512]{0,2,1:T(8,128)(2,1)} %bitcast.264), calls=%async_computation.3 | async-start | bytes 2097152 | tf_op jit(solution)/shard_map/all_to_all | solution.py:69
  48.6 12.5 %all-to-all-done.3 = bf16[128,8,512]{0,2,1:T(8,128)(2,1)} async-done(((bf16[128,8,512]{0,2,1:T(8,128)(2,1)}), bf16[128,8,512]{0,2,1:T(8,128)(2,1)}, u32[]{:S(2)}, u32[]{:S(2)}) %all-to-all-start.3) | async-done | bytes 1048608 | tf_op jit(solution)/shard_map/all_to_all | solution.py:69
  61.1 5.4 %all-to-all-start.2 = ((bf16[128,8,128]{2,0,1:T(8,128)(2,1)}), bf16[128,8,128]{2,0,1:T(8,128)(2,1)}, u32[]{:S(2)}, u32[]{:S(2)}) async-start(bf16[128,8,128]{2,0,1:T(8,128)(2,1)} %copy_bitcast_fusion), calls=%async_computation.2 | async-start | bytes 524288 | tf_op jit(solution)/shard_map/all_to_all | solution.py:71
  67.1 1.3 copy.48
  68.4 2.3 copy.52
  70.7 2.8 all-to-all-done.2
  73.6 134.4 %while.12 = (s32[]{:T(128)}, bf16[2,512,128]{2,1,0:T(8,128)(2,1)}, bf16[2,512,128]{2,1,0:T(8,128)(2,1)}, bf16[2,512,512]{2,1,0:T(8,128)(2,1)}, s32[2,512]{1,0:T(...) while((s32[]{:T(128)}, bf16[2,512,128]{2,1,0:T(8,128)(2,1)}, ...), condition=%wide.region_4.5_spmd, body=%wide.region_0.4_spmd.sunk | while | flops 1109019648 | bytes 93070192 | solution.py:82
  74.3 3.5 gather_fusion.1
  77.9 1.8 gather_fusion
  79.7 1.8 gather_fusion.2
  81.7 3.5 gather_fusion.3
  85.3 1.8 gather_fusion.4
  87.2 3.5 gather_fusion.5
  90.8 1.8 gather_fusion.6
  92.7 3.5 gather_fusion.7
  96.2 1.8 gather_fusion.8
  98.2 3.5 gather_fusion.9
  101.7 1.8 gather_fusion.10
  103.7 3.5 gather_fusion.11
  107.2 1.8 gather_fusion.12
  109.2 3.5 gather_fusion.13
  112.7 1.8 gather_fusion.14
  114.7 3.5 gather_fusion.15
  118.2 1.8 gather_fusion.16
  121.9 1.1 constant_dynamic-slice_fusion.7
  123.2 1.9 fusion.81
  125.1 2.0 copy-done.1
  129.2 4.2 fusion.84
  133.4 1.9 fusion.85
  135.5 3.7 fusion.83
  141.4 3.5 gather_fusion.1
  145.0 1.8 gather_fusion
  146.9 1.8 gather_fusion.2
  148.9 3.5 gather_fusion.3
  152.4 1.8 gather_fusion.4
  154.4 3.5 gather_fusion.5
  157.9 1.8 gather_fusion.6
  159.9 3.5 gather_fusion.7
  163.4 1.8 gather_fusion.8
  165.4 3.5 gather_fusion.9
  168.9 1.8 gather_fusion.10
  170.9 3.5 gather_fusion.11
  174.4 1.8 gather_fusion.12
  176.3 3.5 gather_fusion.13
  179.9 1.8 gather_fusion.14
  181.8 3.5 gather_fusion.15
  185.4 1.8 gather_fusion.16
  190.4 1.9 fusion.81
  192.2 2.0 copy-done.1
  196.3 4.3 fusion.84
  200.6 1.9 fusion.85
  202.7 3.7 fusion.83
  207.9 1.1 copy.56
  209.3 30.2 %all_to_all.88 = bf16[8,1024,128]{1,2,0:T(8,128)(2,1)S(1)} all-to-all(bf16[8,1024,128]{1,2,0:T(8,128)(2,1)S(1)} %stack.3), channel_id=1, replica_groups=mesh['dp'=64,'head'=8] {'head'}, dimensions={0} | all-to-all | bytes 4194304 | tf_op jit(solution)/shard_map/all_to_all | solution.py:86
  239.5 4.3 fusion.51
  244.8 11.3 %all_to_all.89 = bf16[8,128,128]{2,1,0:T(8,128)(2,1)S(1)} all-to-all(bf16[8,128,128]{2,1,0:T(8,128)(2,1)S(1)} %bitcast.269), channel_id=1, replica_groups=mesh['dp'=64,'head'=8] {'head'}, dimensions={0} | all-to-all | bytes 524288 | tf_op jit(solution)/shard_map/all_to_all | solution.py:96
  257.1 225.9 %reduce-scatter.2.cloned.1.call-done = f32[16,1024]{1,0:T(8,128)} async-done(((f32[1024,1024]{1,0:T(8,128)}), f32[16,1024]{1,0:T(8,128)}) %reduce-scatter.2.cloned.1.call-update) | async-done | bytes 65552 | tf_op jit(solution)/shard_map/reduce_scatter | solution.py:88
  (124 shorter events, 21.0 us)
Async XLA Ops:
  7.2 232.3 %copy-start = (bf16[1024,1024]{1,0:T(8,128)(2,1)S(1)}, bf16[1024,1024]{1,0:T(8,128)(2,1)}, u32[]{:S(2)}) copy-start(bf16[1024,1024]{1,0:T(8,128)(2,1)} %param.9) | copy-start | bytes 6291460
  9.0 16.8 %all-to-all-start.1 = ((bf16[128,8,128]{2,0,1:T(8,128)(2,1)}), bf16[128,8,128]{2,0,1:T(8,128)(2,1)}, u32[]{:S(2)}, u32[]{:S(2)}) async-start(bf16[128,8,128]{2,0,1:T(8,128)(2,1)} %copy_bitcast_fusion.1), calls=%async_computation.1 | async-start | bytes 524288 | tf_op jit(solution)/shard_map/all_to_all | solution.py:70
  18.7 29.1 %copy-start.5 = (bf16[128,1024]{1,0:T(8,128)(2,1)S(1)}, bf16[128,1024]{1,0:T(8,128)(2,1)}, u32[]{:S(2)}) copy-start(bf16[128,1024]{1,0:T(8,128)(2,1)} %param.12) | copy-start | bytes 786436
  21.1 45.5 %copy-start.9 = (s32[1024]{0:T(1024)S(1)}, s32[1024]{0:T(1024)}, u32[]{:S(2)}) copy-start(s32[1024]{0:T(1024)} %param.14) | copy-start | bytes 12292
  25.8 16.3 %all-to-all-start = ((bf16[128,8,512]{0,2,1:T(8,128)(2,1)}), bf16[128,8,512]{0,2,1:T(8,128)(2,1)S(1)}, u32[]{:S(2)}, u32[]{:S(2)}) async-start(bf16[128,8,512]{0,2,1:T(8,128)(2,1)} %bitcast.263), calls=%async_computation | async-start | bytes 2097152 | tf_op jit(solution)/shard_map/all_to_all | solution.py:68
  33.4 40.2 %copy-start.10 = (s32[2]{0:T(128)S(1)}, s32[2]{0:T(128)}, u32[]{:S(2)}) copy-start(s32[2]{0:T(128)} %param.15) | copy-start | bytes 28
  42.2 19.0 %all-to-all-start.3 = ((bf16[128,8,512]{0,2,1:T(8,128)(2,1)}), bf16[128,8,512]{0,2,1:T(8,128)(2,1)}, u32[]{:S(2)}, u32[]{:S(2)}) async-start(bf16[128,8,512]{0,2,1:T(8,128)(2,1)} %bitcast.264), calls=%async_computation.3 | async-start | bytes 2097152 | tf_op jit(solution)/shard_map/all_to_all | solution.py:69
  61.1 12.4 %all-to-all-start.2 = ((bf16[128,8,128]{2,0,1:T(8,128)(2,1)}), bf16[128,8,128]{2,0,1:T(8,128)(2,1)}, u32[]{:S(2)}, u32[]{:S(2)}) async-start(bf16[128,8,128]{2,0,1:T(8,128)(2,1)} %copy_bitcast_fusion), calls=%async_computation.2 | async-start | bytes 524288 | tf_op jit(solution)/shard_map/all_to_all | solution.py:71
  66.5 416.5 %reduce-scatter.2.cloned.1.call-start = ((), (), s32[]{:S(2)}) async-start(), calls=%async_computation.7 | async-start | bytes 4259840 | tf_op jit(solution)/shard_map/reduce_scatter | solution.py:88
  123.2 4.9 copy-start.4
  125.0 2.0 copy-start.1
  129.2 4.2 copy-start.2
  133.4 2.1 copy-start.3
  135.5 3.8 copy-start.6
  135.5 5.2 %copy-start.11 = (s32[2]{0:T(128)S(1)}, s32[2]{0:T(128)}, u32[]{:S(2)}) copy-start(s32[2]{0:T(128)} %get-tuple-element.220) | copy-start | bytes 28 | tf_op jit(solution)/shard_map/while
  140.0 0.7 copy-start.7
  190.4 4.9 %copy-start.4 = (bf16[2,512,512]{2,1,0:T(8,128)(2,1)S(1)}, bf16[2,512,512]{2,1,0:T(8,128)(2,1)}, u32[]{:S(2)}) copy-start(bf16[2,512,512]{2,1,0:T(8,128)(2,1)} %get-tuple-element.199) | copy-start | bytes 3145732 | tf_op jit(solution)/shard_map/while
  192.2 2.0 copy-start.1
  196.3 4.3 copy-start.2
  200.6 2.1 copy-start.3
  202.7 3.8 copy-start.6
  202.7 5.2 %copy-start.11 = (s32[2]{0:T(128)S(1)}, s32[2]{0:T(128)}, u32[]{:S(2)}) copy-start(s32[2]{0:T(128)} %get-tuple-element.220) | copy-start | bytes 28 | tf_op jit(solution)/shard_map/while
  207.2 0.7 copy-start.7
  243.8 0.9 copy-start.8
Sparse Core Ops, SparseCore 0:
  244.0 239.0 reduce-scatter.1
